TPU v7x, 32 devices: a whole 2x2x4 slice. The times are simulated.
32 devices in a mesh: gx: 4 (over y, x), gy: 8 (over z, core).
Axes of the slice: x: 2, y: 2, z: 4, core: 2. Of those that a mesh axis runs over, the one named last changes fastest.
Arguments:
- layer_in: bfloat16 [16384, 768], P(('gx', 'gy')), may hold values from -6 to 6
- doc_ids: int32 [32, 512], P('gx'), may hold values from 0 to 7, never falling along the last dimension, each value on 1 to 128 neighbouring positions
- mix_gain: bfloat16 [768], P(('gx', 'gy')), may hold values from 0.5 to 1.5
- value_weight: bfloat16 [768, 768], P('gx', 'gy'), may hold values from -0.21875 to 0.21875
- mixing: bfloat16 [12, 512, 512], P(None, 'gy', 'gx'), may hold values from -9 to 9
- output_weight: bfloat16 [768, 768], P('gy', 'gx'), may hold values from -0.875 to 0.875
- ffn_gain: bfloat16 [768], P(('gx', 'gy')), may hold values from 0.5 to 1.5
- up_weight: bfloat16 [768, 3072], P('gx', 'gy'), may hold values from -0.21875 to 0.21875
- down_weight: bfloat16 [3072, 768], P('gy', 'gx'), may hold values from -0.109375 to 0.109375
- cotangent: bfloat16 [16384, 768], P(('gx', 'gy')), may hold values from -6 to 6
Outputs:
- layer_out: bfloat16 [16384, 768], P(('gx', 'gy'))
- grad_in: float32 [16384, 768], P(('gx', 'gy'))
- grad_mix_gain: float32 [768], P(('gx', 'gy'))
- grad_value: float32 [768, 768], P('gx', 'gy')
- grad_mixing: float32 [12, 512, 512], P(None, 'gy', 'gx')
- grad_output: float32 [768, 768], P('gy', 'gx')
- grad_ffn_gain: float32 [768], P(('gx', 'gy'))
- grad_up: float32 [768, 3072], P('gx', 'gy')
- grad_down: float32 [3072, 768], P('gy', 'gx')
Inputs may be any that keep to these rules, and one draw needn't show every extreme that they name: `doc_ids`: each row packs documents: ids never fall along the row, every id from 0 to 7 holds 1 to 128 tokens, and one document holds exactly 128.
All inputs are finite; a program needn't handle non-finite values.
Results may differ from a plain program's by a relative error of at most 0.025.
Values may be sent and summed in bfloat16 or wider, within the bound.
No kernel may reach another device: no remote copies, remote signals or barrier semaphores. Data moves between devices by JAX's collectives and lax.ppermute only.
A program may use at most 320 MiB of HBM per device.

v0:
```python
import math
import jax
import jax.numpy as jnp
from jax import lax
from jax.sharding import PartitionSpec as P

HS = 64
EPS = 1e-05
NEG = -1e30


def layer_norm(tok_rows, norm_gain):
    average = jnp.mean(tok_rows, axis=-1, keepdims=True)
    centred = tok_rows - average
    spread = jnp.mean(centred * centred, axis=-1, keepdims=True)
    return centred * lax.rsqrt(spread + EPS) * norm_gain


def gelu_tanh(up_vals):
    return jax.nn.gelu(up_vals, approximate=True)


def matmul(left, right):
    return jnp.dot(left, right, preferred_element_type=jnp.float32)


def matmul_nt(left, right):
    return lax.dot_general(
        left, right, (((1,), (1,)), ((), ())), preferred_element_type=jnp.float32
    )


def matmul_tn(left, right):
    return lax.dot_general(
        left, right, (((0,), (0,)), ((), ())), preferred_element_type=jnp.float32
    )


def masked_scores(doc_rows, heads_mix):
    same_doc = doc_rows[:, :, None] == doc_rows[:, None, :]
    return jnp.where(same_doc[:, None], heads_mix[None], NEG)


def to_groups(columns, select):
    return columns[:, None, :] * select[None]


def from_groups(grouped):
    return jnp.sum(grouped, axis=1)


def column_heads(col_width, head_total, head_size):
    col_start = lax.axis_index("gy") * col_width
    head_count = min(head_total, (col_width - 1) // head_size + 2)
    head_start = jnp.minimum(col_start // head_size, head_total - head_count)
    owner = (col_start + jnp.arange(col_width, dtype=jnp.int32)) // head_size - head_start
    select = (owner[None, :] == jnp.arange(head_count, dtype=jnp.int32)[:, None]).astype(
        jnp.bfloat16
    )
    return (head_start, head_count, select)


def mixer_forward(grouped, doc_rows, heads_mix):
    seq_count, length = doc_rows.shape
    groups, group_width = (grouped.shape[1], grouped.shape[2])
    per_block = math.gcd(seq_count, 8)
    blocks = seq_count // per_block
    vals_blocks = grouped.reshape(blocks, per_block, length, groups, group_width)
    doc_blocks = doc_rows.reshape(blocks, per_block, length)

    def block_fn(block_item):
        block_docs, block_vals = block_item
        scores = masked_scores(block_docs, heads_mix)
        row_top = jnp.max(scores, axis=-1, keepdims=True)
        expo_vals = jnp.exp(scores - row_top)
        row_total = jnp.sum(expo_vals, axis=-1, keepdims=True)
        mix_probs = (expo_vals / row_total).astype(jnp.bfloat16)
        mix_out = jnp.einsum(
            "sgqk,skgw->sqgw", mix_probs, block_vals, preferred_element_type=jnp.float32
        )
        return (mix_out, (row_top + jnp.log(row_total))[..., 0])

    mix_out, log_sums = lax.map(block_fn, (doc_blocks, vals_blocks))
    return (mix_out.reshape(seq_count * length, groups, group_width), log_sums)


def mixer_backward(grouped, grad_groups, doc_rows, log_sums, heads_mix):
    seq_count, length = doc_rows.shape
    groups, group_width = (grouped.shape[1], grouped.shape[2])
    per_block = math.gcd(seq_count, 8)
    blocks = seq_count // per_block
    vals_blocks = grouped.reshape(blocks, per_block, length, groups, group_width)
    grad_blocks = grad_groups.reshape(blocks, per_block, length, groups, group_width)
    doc_blocks = doc_rows.reshape(blocks, per_block, length)

    def block_fn(mix_acc, block_item):
        block_docs, block_vals, block_grads, block_sums = block_item
        scores = masked_scores(block_docs, heads_mix)
        mix_probs = jnp.exp(scores - block_sums[..., None])
        vals_grad = jnp.einsum(
            "sgqk,sqgw->skgw",
            mix_probs.astype(jnp.bfloat16),
            block_grads,
            preferred_element_type=jnp.float32,
        )
        probs_grad = jnp.einsum(
            "sqgw,skgw->sgqk", block_grads, block_vals, preferred_element_type=jnp.float32
        )
        score_grad = mix_probs * (
            probs_grad - jnp.sum(mix_probs * probs_grad, axis=-1, keepdims=True)
        )
        return (mix_acc + jnp.sum(score_grad, axis=0), vals_grad)

    mix_init = jnp.zeros(heads_mix.shape, jnp.float32)
    mix_grad, vals_grad = lax.scan(
        block_fn, mix_init, (doc_blocks, vals_blocks, grad_blocks, log_sums)
    )
    return (vals_grad.reshape(seq_count * length, groups, group_width), mix_grad)


def shards(
    layer_in,
    doc_ids,
    mix_gain,
    value_weight,
    mixing,
    output_weight,
    ffn_gain,
    up_weight,
    down_weight,
    cotangent,
):
    mixing_part, gain_one_part, gain_two_part = (
        lax.all_gather(mixing, "gy", axis=1, tiled=True),
        lax.all_gather(mix_gain, "gy", axis=0, tiled=True),
        lax.all_gather(ffn_gain, "gy", axis=0, tiled=True),
    )
    value_cols, up_cols, output_rows, down_rows, mix_full, gain_one, gain_two = (
        lax.all_gather(value_weight, "gx", axis=0, tiled=True),
        lax.all_gather(up_weight, "gx", axis=0, tiled=True),
        lax.all_gather(output_weight, "gx", axis=1, tiled=True),
        lax.all_gather(down_weight, "gx", axis=1, tiled=True),
        lax.all_gather(mixing_part, "gx", axis=2, tiled=True),
        lax.all_gather(gain_one_part, "gx", axis=0, tiled=True),
        lax.all_gather(gain_two_part, "gx", axis=0, tiled=True),
    )
    gain_one = gain_one.astype(jnp.float32)
    gain_two = gain_two.astype(jnp.float32)
    layer_vals = layer_in.astype(jnp.float32)
    cot_vals = cotangent.astype(jnp.float32)
    normed_low = layer_norm(layer_vals, gain_one).astype(jnp.bfloat16)
    normed_all = lax.all_gather(normed_low, "gy", axis=0, tiled=True)
    head_start, head_count, select = column_heads(value_cols.shape[1], mix_full.shape[0], HS)
    heads_mix = lax.dynamic_slice_in_dim(mix_full, head_start, head_count, 0).astype(jnp.float32)
    value_low = matmul(normed_all, value_cols).astype(jnp.bfloat16)
    grouped = to_groups(value_low, select)
    mix_out, log_sums = mixer_forward(grouped, doc_ids, heads_mix)
    mixed_low = from_groups(mix_out).astype(jnp.bfloat16)
    middle = layer_vals + lax.psum_scatter(
        matmul(mixed_low, output_rows), "gy", scatter_dimension=0, tiled=True
    )
    normed_two = layer_norm(middle, gain_two).astype(jnp.bfloat16)
    normed_two_all = lax.all_gather(normed_two, "gy", axis=0, tiled=True)
    up_vals = matmul(normed_two_all, up_cols)
    act_low = gelu_tanh(up_vals).astype(jnp.bfloat16)
    layer_out = (
        middle
        + lax.psum_scatter(
            matmul(act_low, down_rows).astype(jnp.bfloat16), "gy", scatter_dimension=0, tiled=True
        ).astype(jnp.float32)
    ).astype(jnp.bfloat16)
    cot_all = lax.all_gather(cotangent, "gy", axis=0, tiled=True)
    down_grad = matmul_tn(act_low, cot_all)
    act_grad = matmul_nt(cot_all, down_rows)
    gelu_out, gelu_back = jax.vjp(gelu_tanh, up_vals)
    up_grad_low = gelu_back(act_grad)[0].astype(jnp.bfloat16)
    up_weight_grad = matmul_tn(normed_two_all, up_grad_low)
    normed_two_grad = lax.psum_scatter(
        matmul_nt(up_grad_low, up_cols).astype(jnp.bfloat16), "gy", scatter_dimension=0, tiled=True
    ).astype(jnp.float32)
    norm_out, norm_back = jax.vjp(layer_norm, middle, gain_two)
    mid_norm_grad, gain_two_grad = norm_back(normed_two_grad)
    mid_grad = cot_vals + mid_norm_grad
    branch_low = mid_grad.astype(jnp.bfloat16)
    branch_all = lax.all_gather(branch_low, "gy", axis=0, tiled=True)
    output_grad = matmul_tn(mixed_low, branch_all)
    mixed_grad_low = matmul_nt(branch_all, output_rows).astype(jnp.bfloat16)
    vals_grad, mix_grad_local = mixer_backward(
        grouped, to_groups(mixed_grad_low, select), doc_ids, log_sums, heads_mix
    )
    value_grad_low = from_groups(vals_grad).astype(jnp.bfloat16)
    value_grad = matmul_tn(normed_all, value_grad_low)
    normed_one_grad = lax.psum_scatter(
        matmul_nt(value_grad_low, value_cols).astype(jnp.bfloat16),
        "gy",
        scatter_dimension=0,
        tiled=True,
    ).astype(jnp.float32)
    mix_grad_full = lax.dynamic_update_slice_in_dim(
        jnp.zeros(mix_full.shape, jnp.float32), mix_grad_local, head_start, 0
    )
    first_out, first_back = jax.vjp(layer_norm, layer_vals, gain_one)
    in_norm_grad, gain_one_grad = first_back(normed_one_grad)
    grad_in = mid_grad + in_norm_grad
    (
        value_grad,
        up_weight_grad,
        output_grad,
        down_grad,
        mix_grad_part,
        gain_one_part_grad,
        gain_two_part_grad,
    ) = (
        lax.psum_scatter(
            value_grad.astype(jnp.bfloat16), "gx", scatter_dimension=0, tiled=True
        ).astype(jnp.float32),
        lax.psum_scatter(
            up_weight_grad.astype(jnp.bfloat16), "gx", scatter_dimension=0, tiled=True
        ).astype(jnp.float32),
        lax.psum_scatter(
            output_grad.astype(jnp.bfloat16), "gx", scatter_dimension=1, tiled=True
        ).astype(jnp.float32),
        lax.psum_scatter(
            down_grad.astype(jnp.bfloat16), "gx", scatter_dimension=1, tiled=True
        ).astype(jnp.float32),
        lax.psum_scatter(
            mix_grad_full.astype(jnp.bfloat16), "gx", scatter_dimension=2, tiled=True
        ).astype(jnp.float32),
        lax.psum_scatter(
            gain_one_grad.astype(jnp.bfloat16), "gx", scatter_dimension=0, tiled=True
        ).astype(jnp.float32),
        lax.psum_scatter(
            gain_two_grad.astype(jnp.bfloat16), "gx", scatter_dimension=0, tiled=True
        ).astype(jnp.float32),
    )
    mix_grad_out, gain_one_out, gain_two_out = (
        lax.psum_scatter(
            mix_grad_part.astype(jnp.bfloat16), "gy", scatter_dimension=1, tiled=True
        ).astype(jnp.float32),
        lax.psum_scatter(
            gain_one_part_grad.astype(jnp.bfloat16), "gy", scatter_dimension=0, tiled=True
        ).astype(jnp.float32),
        lax.psum_scatter(
            gain_two_part_grad.astype(jnp.bfloat16), "gy", scatter_dimension=0, tiled=True
        ).astype(jnp.float32),
    )
    return (
        layer_out,
        grad_in,
        gain_one_out,
        value_grad,
        mix_grad_out,
        output_grad,
        gain_two_out,
        up_weight_grad,
        down_grad,
    )


def solution(mesh):
    in_specs = (
        P(("gx", "gy"), None),
        P("gx", None),
        P(("gx", "gy")),
        P("gx", "gy"),
        P(None, "gy", "gx"),
        P("gy", "gx"),
        P(("gx", "gy")),
        P("gx", "gy"),
        P("gy", "gx"),
        P(("gx", "gy"), None),
    )
    out_specs = (
        P(("gx", "gy"), None),
        P(("gx", "gy"), None),
        P(("gx", "gy")),
        P("gx", "gy"),
        P(None, "gy", "gx"),
        P("gy", "gx"),
        P(("gx", "gy")),
        P("gx", "gy"),
        P("gy", "gx"),
    )
    return jax.shard_map(shards, mesh=mesh, in_specs=in_specs, out_specs=out_specs, check_vma=False)
```

profile of v0, /device:TPU:0, one launch (start us, length us, event | category | flops | bytes accessed | tf_op | source)
XLA Modules:
  0.0 1063.9 jit_solution(16108159190764218038)
XLA Ops:
  8.0 1.3 fusion.101
  12.4 18.4 %all-reduce.9 = (bf16[192]{0:T(256)(128)(2,1)S(1)}, bf16[192]{0:T(256)(128)(2,1)S(1)}) all-reduce(bf16[192]{0:T(256)(128)(2,1)S(1)} %dynamic-update-slice, bf16[192]{0:T(256)(128)(2,1)S(1)} %dynamic-update-slice.2), channel_id=1, replica_groups=mesh['gx'=4,'gy'=8] {'gy'}, use_global_device_ids=true, to_apply=%add | all-reduce | flops 384 | bytes 1536
  31.2 9.9 all-reduce.11
  42.4 1.5 fusion.57
  44.0 2.3 fusion.53
  47.3 8.2 all_gather.48
  55.5 8.3 all_gather.47
  63.8 1.5 broadcast_compare_fusion
  65.2 42.3 %all-gather.11.cloned.1.call-done = bf16[4096,768]{1,0:T(8,128)(2,1)} async-done(((bf16[512,768]{1,0:T(8,128)(2,1)}), bf16[4096,768]{1,0:T(8,128)(2,1)}) %all-gather.11.cloned.1.call-update) | async-done | bytes 6291472 | tf_op jit(solution)/shard_map/all_gather | solution.py:152
  107.5 4.8 convolution_convert_fusion.4
  113.4 64.7 %all-gather.9.cloned.1.call-done = bf16[12,512,512]{2,1,0:T(8,128)(2,1)} async-done(((bf16[12,512,128]{2,1,0:T(8,128)(2,1)}), bf16[12,512,512]{2,1,0:T(8,128)(2,1)}) %all-gather.9.cloned.1.call-update) | async-done | bytes 6291472 | tf_op jit(solution)/shard_map/all_gather | solution.py:143
  178.1 3.6 dynamic-slice_convert_fusion
  181.6 4.0 copy.31
  185.6 4.3 select_reduce_fusion
  190.0 4.8 fusion.3
  194.8 7.5 fusion.72
  202.4 6.4 fusion.103
  209.5 128.7 %reduce-scatter.15.cloned.1.call-done = f32[512,768]{1,0:T(8,128)} async-done(((f32[4096,768]{1,0:T(8,128)}), f32[512,768]{1,0:T(8,128)}) %reduce-scatter.15.cloned.1.call-update) | async-done | bytes 1572880 | tf_op jit(solution)/shard_map/reduce_scatter | solution.py:159
  338.2 1.6 fusion.100
  341.4 11.7 %all_gather.52 = bf16[768,384]{1,0:T(8,128)(2,1)} all-gather(bf16[192,384]{1,0:T(8,128)(2,1)S(1)} %copy-done.14), channel_id=1, replica_groups=mesh['gx'=4,'gy'=8] {'gx'}, dimensions={0}, use_global_device_ids=true | all-gather | bytes 737280 | tf_op jit(solution)/shard_map/all_gather | solution.py:140
  353.2 10.3 all_gather.53
  363.5 39.3 %all-gather.15.cloned.1.call-done = bf16[4096,768]{1,0:T(8,128)(2,1)} async-done(((bf16[512,768]{1,0:T(8,128)(2,1)}), bf16[4096,768]{1,0:T(8,128)(2,1)}) %all-gather.15.cloned.1.call-update) | async-done | bytes 6291472 | tf_op jit(solution)/shard_map/all_gather | solution.py:172
  402.8 8.9 fusion.104
  411.7 56.6 %all-gather.13.cloned.1.call-done = bf16[4096,768]{1,0:T(8,128)(2,1)} async-done(((bf16[512,768]{1,0:T(8,128)(2,1)}), bf16[4096,768]{1,0:T(8,128)(2,1)}) %all-gather.13.cloned.1.call-update) | async-done | bytes 6291472 | tf_op jit(solution)/shard_map/all_gather | solution.py:163
  468.4 13.7 %fusion.31 = (bf16[4096,384]{1,0:T(8,128)(2,1)S(1)}, f32[4096,384]{1,0:T(8,128)}) fusion(f32[4096,384]{1,0:T(8,128)} %fusion.104, bf16[4096,768]{1,0:T(8,128)(2,1)} %all-gather.13.cloned.1.call-done, bf16[768,384]{1,0:T(8,128)(2,1)} %all_gather.52), kind=kOutput, calls=%fused_computation.36 | convolution fusion | flops 2447376384 | bytes 22609920 | tf_op jit(solution)/shard_map/dot_general | solution.py:24
  482.1 1.6 copy-done.27
  483.7 5.4 convolution_convert_fusion.1
  489.1 9.9 convolution_convert_fusion.2
  499.1 58.6 %reduce-scatter.19.cloned.1.call-done = bf16[512,768]{1,0:T(8,128)(2,1)} async-done(((bf16[4096,768]{1,0:T(8,128)(2,1)}), bf16[512,768]{1,0:T(8,128)(2,1)}) %reduce-scatter.19.cloned.1.call-update) | async-done | bytes 786448 | tf_op jit(solution)/shard_map/reduce_scatter | solution.py:178
  557.7 1.8 fusion.55
  559.5 68.6 %reduce-scatter.17.cloned.1.call-done = bf16[512,768]{1,0:T(8,128)(2,1)} async-done(((bf16[4096,768]{1,0:T(8,128)(2,1)}), bf16[512,768]{1,0:T(8,128)(2,1)}) %reduce-scatter.17.cloned.1.call-update) | async-done | bytes 786448 | tf_op jit(solution)/shard_map/reduce_scatter | solution.py:168
  628.2 2.9 fusion.99
  634.0 62.8 %all-gather.17.cloned.1.call-done = bf16[4096,768]{1,0:T(8,128)(2,1)} async-done(((bf16[512,768]{1,0:T(8,128)(2,1)}), bf16[4096,768]{1,0:T(8,128)(2,1)}) %all-gather.17.cloned.1.call-update) | async-done | bytes 6291472 | tf_op jit(solution)/shard_map/all_gather | solution.py:185
  696.7 4.8 convolution_convert_fusion.3
  702.6 16.4 %fusion = f32[8,3,512,512]{2,3,1,0:T(8,128)} fusion(f32[8,3,512]{2,1,0:T(4,128)S(1)} %log_add_fusion, f32[3,512,512]{1,2,0:T(8,128)} %copy.31, pred[8,512,512]{1,2,0:T(8,128)(4,1)S(1)} %copy-done.5, bf16[8,512,96]{1,2,0:T(8,128)(2,1)} %bitcast.68, bf16[3,96]{1,0:T(4,128)(2,1)S(1)} %fusion.92, bf16[8,512,96]{1,2,0:T(8,128)(2,1)} %bitcast.65), kind=kOutput, calls=%fused_computation | convolution fusion | flops 1229206016 | bytes 32031296 | tf_op jit(solution)/shard_map/while/body/eval_jaxpr/sub | solution.py:110
  719.0 15.5 %fusion.9 = bf16[3,512,512]{1,2,0:T(8,128)(2,1)} fusion(f32[8,3,512,512]{2,3,1,0:T(8,128)} %fusion, f32[8,3,512]{2,1,0:T(4,128)S(1)} %log_add_fusion, f32[3,512,512]{1,2,0:T(8,128)} %copy.31, pred[8,512,512]{1,2,0:T(8,128)(4,1)S(1)} %copy-done.5, bf16[3,96]{1,0:T(4,128)(2,1)S(1)} %fusion.92, bf16[8,512,96]{1,2,0:T(8,128)(2,1)} %bitcast.66, ...), kind=kOutput, calls=%fused_computation.12 | convolution fusion | flops 1240989696 | bytes 33604160 | tf_op jit(solution)/shard_map/while/body/eval_jaxpr/sqgw,skgw->sgqk/dot_general | solution.py:106
  734.4 2.6 copy.39
  737.1 3.2 broadcast_in_dim.115
  741.6 14.6 %copy.44 = bf16[12,512,512]{1,0,2:T(8,128)(2,1)} copy(bf16[12,512,512]{2,1,0:T(8,128)(2,1)} %constant_dynamic-update-slice_fusion) | data formatting | bytes 12582912
  756.2 13.4 %copy.52 = bf16[64,8,12,512]{3,1,2,0:T(8,128)(2,1)} copy(bf16[64,8,12,512]{3,2,1,0:T(8,128)(2,1)} %bitcast.56) | data formatting | bytes 12582912
  769.7 8.9 convolution_convert_fusion.5
  778.9 8.0 convolution_convert_fusion.6
  787.0 4.3 convolution_convert_fusion.8
  792.2 9.2 fusion.67
  802.7 5.5 convolution_convert_fusion.7
  808.5 4.5 convolution_convert_fusion
  813.0 25.6 %reduce-scatter.31.cloned.1.call-done = bf16[128,6144]{1,0:T(8,128)(2,1)} async-done(((bf16[512,6144]{1,0:T(8,128)(2,1)}), bf16[128,6144]{1,0:T(8,128)(2,1)}) %reduce-scatter.31.cloned.1.call-update) | async-done | bytes 1572880
  838.6 2.9 reshape.182
  841.5 2.9 copy.45
  845.8 20.7 %reduce-scatter.29.cloned.1.call-done = bf16[384,192]{0,1:T(8,128)(2,1)} async-done(((bf16[384,768]{0,1:T(8,128)(2,1)}), bf16[384,192]{0,1:T(8,128)(2,1)}) %reduce-scatter.29.cloned.1.call-update) | async-done | bytes 147472 | tf_op jit(solution)/shard_map/reduce_scatter | solution.py:223
  866.6 1.6 convert_element_type.171
  868.2 26.4 %reduce-scatter.27.cloned.1.call-done = bf16[192,384]{1,0:T(8,128)(2,1)} async-done(((bf16[768,384]{1,0:T(8,128)(2,1)}), bf16[192,384]{1,0:T(8,128)(2,1)}) %reduce-scatter.27.cloned.1.call-update) | async-done | bytes 147472 | tf_op jit(solution)/shard_map/reduce_scatter | solution.py:217
  894.7 1.6 convert_element_type.169
  896.3 25.1 %reduce-scatter.33.cloned.1.call-done = bf16[192,96]{1,0:T(8,128)(2,1)} async-done(((bf16[768,96]{1,0:T(8,128)(2,1)}), bf16[192,96]{1,0:T(8,128)(2,1)}) %reduce-scatter.33.cloned.1.call-update) | async-done | bytes 36880
  923.0 25.7 %reduce-scatter.23.cloned.1.call-done = bf16[192,96]{1,0:T(8,128)(2,1)} async-done(((bf16[768,96]{1,0:T(8,128)(2,1)}), bf16[192,96]{1,0:T(8,128)(2,1)}) %reduce-scatter.23.cloned.1.call-update) | async-done | bytes 36880 | tf_op jit(solution)/shard_map/reduce_scatter | solution.py:214
  948.6 1.4 convert_element_type.161
  950.1 70.5 %reduce-scatter.21.cloned.1.call-done = bf16[512,768]{1,0:T(8,128)(2,1)} async-done(((bf16[4096,768]{1,0:T(8,128)(2,1)}), bf16[512,768]{1,0:T(8,128)(2,1)}) %reduce-scatter.21.cloned.1.call-update) | async-done | bytes 786448 | tf_op jit(solution)/shard_map/reduce_scatter | solution.py:193
  1020.6 1.7 fusion.58
  1022.3 2.1 fusion.56
  1024.4 9.8 all-reduce.10
  1034.4 13.7 %all-reduce.8 = (bf16[192]{0:T(256)(128)(2,1)S(1)}, bf16[192]{0:T(256)(128)(2,1)S(1)}) all-reduce(bf16[192]{0:T(256)(128)(2,1)S(1)} %dynamic-slice.6, bf16[192]{0:T(256)(128)(2,1)S(1)} %dynamic-slice.10), channel_id=7, replica_groups=mesh['gx'=4,'gy'=8] {'gy'}, use_global_device_ids=true, to_apply=%region_16.17.clone | all-reduce | flops 384 | bytes 1536
  1049.3 3.0 add_add_fusion.2
  1052.3 3.2 reduce-scatter.25.cloned.1.call-done
  1055.4 1.7 convert_element_type.163
  (126 shorter events, 19.5 us)
Async XLA Ops:
  7.2 40.0 %copy-start.21 = (bf16[96,192]{1,0:T(8,128)(2,1)S(1)}, bf16[96,192]{1,0:T(8,128)(2,1)}, u32[]{:S(2)}) copy-start(bf16[96,192]{1,0:T(8,128)(2,1)} %param.15) | copy-start | bytes 110596
  7.2 48.3 %copy-start.22 = (bf16[192,96]{1,0:T(8,128)(2,1)S(1)}, bf16[192,96]{1,0:T(8,128)(2,1)}, u32[]{:S(2)}) copy-start(bf16[192,96]{1,0:T(8,128)(2,1)} %param.13) | copy-start | bytes 110596
  7.2 39.2 %all-gather.7.cloned.1.call-start = ((), (), s32[]{:S(2)}) async-start(), calls=%async_computation.10 | async-start | bytes 1769472 | tf_op jit(solution)/shard_map/all_gather | solution.py:134
  7.9 55.8 %copy-start.20 = (s32[8,512]{1,0:T(8,128)S(1)}, s32[8,512]{1,0:T(8,128)}, u32[]{:S(2)}) copy-start(s32[8,512]{1,0:T(8,128)} %param.11) | copy-start | bytes 49156
  7.9 99.6 %all-gather.11.cloned.1.call-start = ((), (), s32[]{:S(2)}) async-start(), calls=%async_computation.12 | async-start | bytes 7077888 | tf_op jit(solution)/shard_map/all_gather | solution.py:152
  41.1 6.0 copy-start.16
  42.4 4.7 copy-start.18
  43.9 3.2 copy-start.25
  43.9 3.2 copy-start.23
  46.3 131.8 %all-gather.9.cloned.1.call-start = ((), (), s32[]{:S(2)}) async-start(), calls=%async_computation.11 | async-start | bytes 7864320 | tf_op jit(solution)/shard_map/all_gather | solution.py:143
  47.0 291.2 %reduce-scatter.15.cloned.1.call-start = ((), (), s32[]{:S(2)}) async-start(), calls=%async_computation.13 | async-start | bytes 14155776 | tf_op jit(solution)/shard_map/reduce_scatter | solution.py:159
  63.7 48.6 %copy-start.10 = (bf16[768,96]{1,0:T(8,128)(2,1)}, bf16[768,96]{1,0:T(8,128)(2,1)S(1)}, u32[]{:S(2)}) copy-start(bf16[768,96]{1,0:T(8,128)(2,1)S(1)} %all_gather.47) | copy-start | bytes 442372
  65.2 129.5 %copy-start.4 = (pred[8,512,512]{1,2,0:T(8,128)(4,1)}, pred[8,512,512]{1,2,0:T(8,128)(4,1)S(1)}, u32[]{:S(2)}) copy-start(pred[8,512,512]{1,2,0:T(8,128)(4,1)S(1)} %broadcast_compare_fusion) | copy-start | bytes 6291460
  185.6 4.3 copy-start.3
  190.0 4.8 copy-start.12
  202.4 6.4 copy-start.6
  208.8 129.4 %copy-start = (bf16[512,768]{1,0:T(8,128)(2,1)S(1)}, bf16[512,768]{1,0:T(8,128)(2,1)}, u32[]{:S(2)}) copy-start(bf16[512,768]{1,0:T(8,128)(2,1)} %param.10) | copy-start | bytes 2359300
  208.8 194.0 %all-gather.15.cloned.1.call-start = ((), (), s32[]{:S(2)}) async-start(), calls=%async_computation.16 | async-start | bytes 7077888 | tf_op jit(solution)/shard_map/all_gather | solution.py:172
  209.4 258.9 %all-gather.13.cloned.1.call-start = ((), (), s32[]{:S(2)}) async-start(), calls=%async_computation.14 | async-start | bytes 7077888 | tf_op jit(solution)/shard_map/all_gather | solution.py:163
  339.8 1.6 copy-start.14
  339.9 13.3 %copy-start.15 = (bf16[384,192]{0,1:T(8,128)(2,1)S(1)}, bf16[384,192]{0,1:T(8,128)(2,1)}, u32[]{:S(2)}) copy-start(bf16[384,192]{0,1:T(8,128)(2,1)} %param.18) | copy-start | bytes 442372
  341.4 216.3 %reduce-scatter.19.cloned.1.call-start = ((), (), s32[]{:S(2)}) async-start(), calls=%async_computation.17 | async-start | bytes 7077888 | tf_op jit(solution)/shard_map/reduce_scatter | solution.py:178
  468.4 15.3 %copy-start.13 = (bf16[768,384]{1,0:T(8,128)(2,1)S(1)}, bf16[768,384]{1,0:T(8,128)(2,1)}, u32[]{:S(2)}) copy-start(bf16[768,384]{1,0:T(8,128)(2,1)} %all_gather.52) | copy-start | bytes 1769476
  482.0 1.6 copy-start.27
  489.1 139.1 %reduce-scatter.17.cloned.1.call-start = ((), (), s32[]{:S(2)}) async-start(), calls=%async_computation.15 | async-start | bytes 7077888 | tf_op jit(solution)/shard_map/reduce_scatter | solution.py:168
  499.0 197.7 %all-gather.17.cloned.1.call-start = ((), (), s32[]{:S(2)}) async-start(), calls=%async_computation.18 | async-start | bytes 7077888 | tf_op jit(solution)/shard_map/all_gather | solution.py:185
  559.5 72.8 %copy-start.8 = (bf16[512,768]{1,0:T(8,128)(2,1)S(1)}, bf16[512,768]{1,0:T(8,128)(2,1)}, u32[]{:S(2)}) copy-start(bf16[512,768]{1,0:T(8,128)(2,1)} %param.19) | copy-start | bytes 2359300
  631.1 1.1 copy-start.1
  633.5 205.2 %reduce-scatter.31.cloned.1.call-start = ((), (), s32[]{:S(2)}) async-start(), calls=%async_computation.24 | async-start | bytes 7864320
  633.9 68.6 %copy-start.5 = (pred[8,512,512]{1,2,0:T(8,128)(4,1)S(1)}, pred[8,512,512]{1,2,0:T(8,128)(4,1)}, u32[]{:S(2)}) copy-start(pred[8,512,512]{1,2,0:T(8,128)(4,1)} %copy-done.4) | copy-start | bytes 6291460
  737.1 3.2 copy-start.9
  769.7 96.9 %reduce-scatter.29.cloned.1.call-start = ((), (), s32[]{:S(2)}) async-start(), calls=%async_computation.23 | async-start | bytes 737280 | tf_op jit(solution)/shard_map/reduce_scatter | solution.py:223
  778.7 116.0 %reduce-scatter.27.cloned.1.call-start = ((), (), s32[]{:S(2)}) async-start(), calls=%async_computation.22 | async-start | bytes 737280 | tf_op jit(solution)/shard_map/reduce_scatter | solution.py:217
  786.9 134.5 %reduce-scatter.33.cloned.1.call-start = ((), (), s32[]{:S(2)}) async-start(), calls=%async_computation.25 | async-start | bytes 245760
  802.6 146.0 %reduce-scatter.23.cloned.1.call-start = ((), (), s32[]{:S(2)}) async-start(), calls=%async_computation.20 | async-start | bytes 245760 | tf_op jit(solution)/shard_map/reduce_scatter | solution.py:214
  802.6 5.8 copy-start.11
  808.2 212.4 %reduce-scatter.21.cloned.1.call-start = ((), (), s32[]{:S(2)}) async-start(), calls=%async_computation.19 | async-start | bytes 7077888 | tf_op jit(solution)/shard_map/reduce_scatter | solution.py:193
  813.0 242.5 %reduce-scatter.25.cloned.1.call-start = ((), (), s32[]{:S(2)}) async-start(), calls=%async_computation.21 | async-start | bytes 1769472 | tf_op jit(solution)/shard_map/reduce_scatter | solution.py:237
  841.5 179.1 %copy-start.17 = (f32[768]{0:T(1024)S(1)}, f32[768]{0:T(1024)}, u32[]{:S(2)}) copy-start(f32[768]{0:T(1024)} %copy-done.16) | copy-start | bytes 9220
  841.5 179.1 %copy-start.19 = (f32[512]{0:T(512)S(1)}, f32[512]{0:T(512)}, u32[]{:S(2)}) copy-start(f32[512]{0:T(512)} %copy-done.18) | copy-start | bytes 6148
  841.5 180.8 %copy-start.26 = (f32[512]{0:T(512)S(1)}, f32[512]{0:T(512)}, u32[]{:S(2)}) copy-start(f32[512]{0:T(512)} %copy-done.25) | copy-start | bytes 6148
  844.4 177.9 %copy-start.24 = (f32[512]{0:T(512)S(1)}, f32[512]{0:T(512)}, u32[]{:S(2)}) copy-start(f32[512]{0:T(512)} %copy-done.23) | copy-start | bytes 6148
  844.4 204.9 %copy-start.2 = (f32[512,768]{1,0:T(8,128)S(1)}, f32[512,768]{1,0:T(8,128)}, u32[]{:S(2)}) copy-start(f32[512,768]{1,0:T(8,128)} %copy-done.1) | copy-start | bytes 4718596
  1020.6 28.7 %copy-start.7 = (bf16[512,768]{1,0:T(8,128)(2,1)S(1)}, bf16[512,768]{1,0:T(8,128)(2,1)}, u32[]{:S(2)}) copy-start(bf16[512,768]{1,0:T(8,128)(2,1)} %reduce-scatter.21.cloned.1.call-done) | copy-start | bytes 2359300
Sparse Core Ops, SparseCore 0:
  9.6 27.8 all-gather.6
  46.4 61.0 all-gather.10
  109.4 68.6 all-gather.8
  208.9 129.2 reduce-scatter.14
  339.7 63.0 all-gather.14
  404.9 63.3 all-gather.12
  489.2 68.4 reduce-scatter.18
  560.0 68.1 reduce-scatter.16
  633.6 63.1 all-gather.16
  769.8 68.8 reduce-scatter.30
  841.5 25.0 reduce-scatter.28
  869.6 25.0 reduce-scatter.26
  897.4 23.9 reduce-scatter.32
  924.6 23.9 reduce-scatter.22
  950.8 69.7 reduce-scatter.20
  1022.8 32.6 reduce-scatter.24
where the time goes:
time: 1070 us; the launch traced here: 1060 us
  waiting for transfers between devices  721 us (67%)
  matrix products  134 us (13%)
  blocking collectives  90.4 us (8%)
  local copies, waits for them, and re-layouts  56.6 us (5%)
  other arithmetic  43.4 us (4%)
  between operations  17.4 us (2%)
    reduce_scatter x1, waiting for transfers between devices, shards(): lax.psum_scatter(matmul(mixed_low, output_rows), 'gy', scatter_dimension=...  129 us
    reduce_scatter x1, waiting for transfers between devices, shards(): lax.psum_scatter(matmul_nt(value_grad_low, value_cols).astype(jnp.bfloat1...  70.5 us
    reduce_scatter x1, waiting for transfers between devices, shards(): lax.psum_scatter(matmul(act_low, down_rows).astype(jnp.bfloat16), 'gy', s...  68.6 us
    all_gather x1, waiting for transfers between devices, shards(): lax.all_gather(mixing_part, 'gx', axis=2, tiled=True)  64.7 us
    all_gather x1, waiting for transfers between devices, shards(): branch_all = lax.all_gather(branch_low, 'gy', axis=0, tiled=True)  62.8 us
    reduce_scatter x1, waiting for transfers between devices, shards(): lax.psum_scatter(matmul_nt(up_grad_low, up_cols).astype(jnp.bfloat16), 'g...  58.6 us
    all_gather x1, waiting for transfers between devices, shards(): normed_two_all = lax.all_gather(normed_two, 'gy', axis=0, tiled=True)  56.6 us
    unnamed x18, waiting for transfers between devices  52.8 us
  transfers between devices with their start and end apart: 16, of which 15 were waited for; matrix products, arithmetic and copies ran while one was open for 10% of the time, Pallas kernels for 0%

commit v1 on v0

--- a/solution.py
+++ b/solution.py
@@ -160,7 +160,12 @@
         matmul(mixed_low, output_rows), "gy", scatter_dimension=0, tiled=True
     )
     normed_two = layer_norm(middle, gain_two).astype(jnp.bfloat16)
-    normed_two_all = lax.all_gather(normed_two, "gy", axis=0, tiled=True)
+    ring = [normed_two]
+    for hop in range(7):
+        ring.append(lax.ppermute(ring[-1], "gy", [(dev, (dev + 1) % 8) for dev in range(8)]))
+    normed_two_all = jnp.roll(
+        jnp.concatenate(ring[::-1], axis=0), (lax.axis_index("gy") + 1) * ring[0].shape[0], axis=0
+    )
     up_vals = matmul(normed_two_all, up_cols)
     act_low = gelu_tanh(up_vals).astype(jnp.bfloat16)
     layer_out = (

time: 1070 us -> 1110 us (1.037)
  waiting for transfers between devices: 721 us -> 739 us
  local copies, waits for them, and re-layouts: 56.6 us -> 69.6 us
    ppermute x0 -> x7, waiting for transfers between devices: none -> 119 us  [shards(): lax.ppermute(ring[-1], 'gy', [(dev, (dev + 1) % 8) for dev in range(8)])]
    all_gather x1 -> x0, waiting for transfers between devices: 56.6 us -> none  [shards(): normed_two_all = lax.all_gather(normed_two, 'gy', axis=0, tiled=True)]
    all_gather x1, waiting for transfers between devices: 39.3 us -> 0.01 us  [shards(): cot_all = lax.all_gather(cotangent, 'gy', axis=0, tiled=True)]
    unnamed x74 -> x100, local copies, waits for them, and re-layouts: 42 us -> 55.4 us
    dot_general x1, matrix products: 7.5 us -> 19.2 us  [block_fn(): jnp.einsum('sgqk,skgw->sqgw', mix_probs, block_vals, preferred_element_ty...]
    unnamed x18 -> x17, waiting for transfers between devices: 52.8 us -> 52.6 us
  transfers between devices with their start and end apart: 16 -> 22, of which waited for: 15 -> 19; matrix products, arithmetic and copies ran while one was open for 10% -> 9% of each run, Pallas kernels for 0% -> 0%
where the time goes in v1:
time: 1110 us; the launch traced here: 1100 us
  waiting for transfers between devices  739 us (67%)
  matrix products  137 us (12%)
  blocking collectives  91.5 us (8%)
  local copies, waits for them, and re-layouts  69.6 us (6%)
  other arithmetic  44.9 us (4%)
  between operations  17.5 us (2%)
    reduce_scatter x1, waiting for transfers between devices, shards(): lax.psum_scatter(matmul(mixed_low, output_rows), 'gy', scatter_dimension=...  129 us
    ppermute x7, waiting for transfers between devices, shards(): lax.ppermute(ring[-1], 'gy', [(dev, (dev + 1) % 8) for dev in range(8)])  119 us
    reduce_scatter x1, waiting for transfers between devices, shards(): lax.psum_scatter(matmul_nt(value_grad_low, value_cols).astype(jnp.bfloat1...  70.5 us
    reduce_scatter x1, waiting for transfers between devices, shards(): lax.psum_scatter(matmul(act_low, down_rows).astype(jnp.bfloat16), 'gy', s...  68.7 us
    all_gather x1, waiting for transfers between devices, shards(): lax.all_gather(mixing_part, 'gx', axis=2, tiled=True)  64.7 us
    all_gather x1, waiting for transfers between devices, shards(): branch_all = lax.all_gather(branch_low, 'gy', axis=0, tiled=True)  63.2 us
    reduce_scatter x1, waiting for transfers between devices, shards(): lax.psum_scatter(matmul_nt(up_grad_low, up_cols).astype(jnp.bfloat16), 'g...  55.9 us
    unnamed x100, local copies, waits for them, and re-layouts  55.4 us
  transfers between devices with their start and end apart: 22, of which 19 were waited for; matrix products, arithmetic and copies ran while one was open for 9% of the time, Pallas kernels for 0%

profile of v1, /device:TPU:0, one launch (start us, length us, event | category | flops | bytes accessed | tf_op | source)
XLA Modules:
  0.0 1101.0 jit_solution(6515213711016294847)
XLA Ops:
  12.3 18.4 %all-reduce.9 = (bf16[192]{0:T(256)(128)(2,1)S(1)}, bf16[192]{0:T(256)(128)(2,1)S(1)}) all-reduce(bf16[192]{0:T(256)(128)(2,1)S(1)} %dynamic-update-slice, bf16[192]{0:T(256)(128)(2,1)S(1)} %dynamic-update-slice.2), channel_id=1, replica_groups=mesh['gx'=4,'gy'=8] {'gy'}, use_global_device_ids=true, to_apply=%add | all-reduce | flops 384 | bytes 1536
  31.2 9.9 all-reduce.11
  44.0 2.3 fusion.57
  48.0 8.4 all_gather.44
  56.4 8.3 all_gather.45
  66.2 41.3 %all-gather.10.cloned.1.call-done = bf16[4096,768]{1,0:T(8,128)(2,1)} async-done(((bf16[512,768]{1,0:T(8,128)(2,1)}), bf16[4096,768]{1,0:T(8,128)(2,1)}) %all-gather.10.cloned.1.call-update) | async-done | bytes 6291472 | tf_op jit(solution)/shard_map/all_gather | solution.py:152
  107.5 4.8 convolution_convert_fusion.4
  113.3 64.7 %all-gather.8.cloned.1.call-done = bf16[12,512,512]{2,1,0:T(8,128)(2,1)} async-done(((bf16[12,512,128]{2,1,0:T(8,128)(2,1)}), bf16[12,512,512]{2,1,0:T(8,128)(2,1)}) %all-gather.8.cloned.1.call-update) | async-done | bytes 6291472 | tf_op jit(solution)/shard_map/all_gather | solution.py:143
  178.1 3.6 dynamic-slice_convert_fusion
  181.7 3.9 copy.31
  185.6 4.2 select_reduce_fusion
  189.7 6.8 fusion.3
  196.6 19.2 %fusion.79 = bf16[8,12,8,512]{3,2,1,0:T(8,128)(2,1)S(1)} fusion(f32[8,3,512]{2,1,0:T(4,128)S(1)} %fusion.3, f32[8,3,512]{2,1,0:T(4,128)S(1)} %select_reduce_fusion, f32[3,512,512]{1,2,0:T(8,128)S(1)} %copy-done.3, pred[8,512,512]{1,2,0:T(8,128)(4,1)S(1)} %broadcast_compare_fusion, bf16[3,96]{1,0:T(4,128)(2,1)S(1)} %fusion.99, ...), kind=kOutput, calls=%fused_computation.84 | convolution fusion | flops 1238237184 | bytes 6914624 | tf_op jit(solution)/shard_map/while/body/eval_jaxpr/sgqk,skgw->sqgw/dot_general | solution.py:78
  215.9 6.4 fusion.112
  222.9 128.7 %reduce-scatter.15.cloned.1.call-done = f32[512,768]{1,0:T(8,128)} async-done(((f32[4096,768]{1,0:T(8,128)}), f32[512,768]{1,0:T(8,128)}) %reduce-scatter.15.cloned.1.call-update) | async-done | bytes 1572880 | tf_op jit(solution)/shard_map/reduce_scatter | solution.py:159
  351.7 1.6 fusion.109
  354.0 19.3 %collective-permute-done = bf16[512,768]{1,0:T(8,128)(2,1)S(1)} collective-permute-done((bf16[512,768]{1,0:T(8,128)(2,1)S(1)}, bf16[512,768]{1,0:T(8,128)(2,1)S(1)}, u32[]{:S(2)}, u32[]{:S(2)}) %collective-permute-start) | collective-permute-done | bytes 786464 | tf_op jit(solution)/shard_map/ppermute | solution.py:165
  373.3 30.1 %collective-permute-done.1 = bf16[512,768]{1,0:T(8,128)(2,1)S(1)} collective-permute-done((bf16[512,768]{1,0:T(8,128)(2,1)S(1)}, bf16[512,768]{1,0:T(8,128)(2,1)S(1)}, u32[]{:S(2)}, u32[]{:S(2)}) %collective-permute-start.1) | collective-permute-done | bytes 786464 | tf_op jit(solution)/shard_map/ppermute | solution.py:165
  404.3 30.0 %collective-permute-done.2 = bf16[512,768]{1,0:T(8,128)(2,1)S(1)} collective-permute-done((bf16[512,768]{1,0:T(8,128)(2,1)S(1)}, bf16[512,768]{1,0:T(8,128)(2,1)S(1)}, u32[]{:S(2)}, u32[]{:S(2)}) %collective-permute-start.2) | collective-permute-done | bytes 786464 | tf_op jit(solution)/shard_map/ppermute | solution.py:165
  435.2 13.2 %collective-permute-done.3 = bf16[512,768]{1,0:T(8,128)(2,1)S(1)} collective-permute-done((bf16[512,768]{1,0:T(8,128)(2,1)S(1)}, bf16[512,768]{1,0:T(8,128)(2,1)S(1)}, u32[]{:S(2)}, u32[]{:S(2)}) %collective-permute-start.3) | collective-permute-done | bytes 786464 | tf_op jit(solution)/shard_map/ppermute | solution.py:165
  449.3 13.2 %collective-permute-done.4 = bf16[512,768]{1,0:T(8,128)(2,1)S(1)} collective-permute-done((bf16[512,768]{1,0:T(8,128)(2,1)S(1)}, bf16[512,768]{1,0:T(8,128)(2,1)S(1)}, u32[]{:S(2)}, u32[]{:S(2)}) %collective-permute-start.4) | collective-permute-done | bytes 786464 | tf_op jit(solution)/shard_map/ppermute | solution.py:165
  463.4 13.3 %collective-permute-done.5 = bf16[512,768]{1,0:T(8,128)(2,1)} collective-permute-done((bf16[512,768]{1,0:T(8,128)(2,1)S(1)}, bf16[512,768]{1,0:T(8,128)(2,1)}, u32[]{:S(2)}, u32[]{:S(2)}) %collective-permute-start.5) | collective-permute-done | bytes 786464 | tf_op jit(solution)/shard_map/ppermute | solution.py:165
  476.7 12.0 %all_gather.49 = bf16[384,768]{0,1:T(8,128)(2,1)} all-gather(bf16[384,192]{0,1:T(8,128)(2,1)} %param.18), channel_id=1, replica_groups=mesh['gx'=4,'gy'=8] {'gx'}, dimensions={1}, use_global_device_ids=true | all-gather | bytes 737280 | tf_op jit(solution)/shard_map/all_gather | solution.py:142
  488.7 11.0 all_gather.48
  499.7 5.8 fusion.113
  511.7 8.6 fusion.31
  520.3 1.6 copy-done.33
  521.9 5.3 convolution_convert_fusion.1
  528.3 10.1 convolution_convert_fusion.2
  538.8 55.9 %reduce-scatter.19.cloned.1.call-done = bf16[512,768]{1,0:T(8,128)(2,1)} async-done(((bf16[4096,768]{1,0:T(8,128)(2,1)}), bf16[512,768]{1,0:T(8,128)(2,1)}) %reduce-scatter.19.cloned.1.call-update) | async-done | bytes 786448 | tf_op jit(solution)/shard_map/reduce_scatter | solution.py:183
  594.8 1.8 fusion.59
  596.7 68.7 %reduce-scatter.17.cloned.1.call-done = bf16[512,768]{1,0:T(8,128)(2,1)} async-done(((bf16[4096,768]{1,0:T(8,128)(2,1)}), bf16[512,768]{1,0:T(8,128)(2,1)}) %reduce-scatter.17.cloned.1.call-update) | async-done | bytes 786448 | tf_op jit(solution)/shard_map/reduce_scatter | solution.py:173
  665.3 2.9 fusion.108
  670.7 63.2 %all-gather.14.cloned.1.call-done = bf16[4096,768]{1,0:T(8,128)(2,1)} async-done(((bf16[512,768]{1,0:T(8,128)(2,1)}), bf16[4096,768]{1,0:T(8,128)(2,1)}) %all-gather.14.cloned.1.call-update) | async-done | bytes 6291472 | tf_op jit(solution)/shard_map/all_gather | solution.py:190
  733.9 4.8 convolution_convert_fusion.3
  739.7 16.4 %fusion = f32[8,3,512,512]{2,3,1,0:T(8,128)} fusion(f32[8,3,512]{2,1,0:T(4,128)S(1)} %log_add_fusion, f32[3,512,512]{1,2,0:T(8,128)} %copy.31, pred[8,512,512]{1,2,0:T(8,128)(4,1)S(1)} %copy-done.5, bf16[8,512,96]{1,2,0:T(8,128)(2,1)} %bitcast.66, bf16[3,96]{1,0:T(4,128)(2,1)S(1)} %fusion.99, bf16[8,512,96]{1,2,0:T(8,128)(2,1)} %bitcast.63), kind=kOutput, calls=%fused_computation | convolution fusion | flops 1229206016 | bytes 32031296 | tf_op jit(solution)/shard_map/while/body/eval_jaxpr/sub | solution.py:110
  756.1 15.4 %fusion.9 = bf16[3,512,512]{1,2,0:T(8,128)(2,1)} fusion(f32[8,3,512,512]{2,3,1,0:T(8,128)} %fusion, f32[8,3,512]{2,1,0:T(4,128)S(1)} %log_add_fusion, f32[3,512,512]{1,2,0:T(8,128)} %copy.31, pred[8,512,512]{1,2,0:T(8,128)(4,1)S(1)} %copy-done.5, bf16[3,96]{1,0:T(4,128)(2,1)S(1)} %fusion.99, bf16[8,512,96]{1,2,0:T(8,128)(2,1)} %bitcast.64, ...), kind=kOutput, calls=%fused_computation.12 | convolution fusion | flops 1240989696 | bytes 33604160 | tf_op jit(solution)/shard_map/while/body/eval_jaxpr/sqgw,skgw->sgqk/dot_general | solution.py:106
  771.5 2.6 copy.39
  774.1 3.2 broadcast_in_dim.115
  778.7 14.6 %copy.44 = bf16[12,512,512]{1,0,2:T(8,128)(2,1)} copy(bf16[12,512,512]{2,1,0:T(8,128)(2,1)} %constant_dynamic-update-slice_fusion.16) | data formatting | bytes 12582912
  793.2 13.4 %copy.52 = bf16[64,8,12,512]{3,1,2,0:T(8,128)(2,1)} copy(bf16[64,8,12,512]{3,2,1,0:T(8,128)(2,1)} %bitcast.54) | data formatting | bytes 12582912
  806.7 8.0 fusion.71
  815.0 9.0 convolution_convert_fusion.5
  824.0 4.4 convolution_convert_fusion.7
  829.2 9.2 fusion.74
  840.0 5.4 convolution_convert_fusion.6
  845.5 4.5 convolution_convert_fusion
  850.2 25.6 %reduce-scatter.31.cloned.1.call-done = bf16[128,6144]{1,0:T(8,128)(2,1)} async-done(((bf16[512,6144]{1,0:T(8,128)(2,1)}), bf16[128,6144]{1,0:T(8,128)(2,1)}) %reduce-scatter.31.cloned.1.call-update) | async-done | bytes 1572880
  875.7 4.0 reshape.182
  879.7 4.3 copy.45
  885.3 18.2 %reduce-scatter.27.cloned.1.call-done = bf16[192,384]{1,0:T(8,128)(2,1)} async-done(((bf16[768,384]{1,0:T(8,128)(2,1)}), bf16[192,384]{1,0:T(8,128)(2,1)}) %reduce-scatter.27.cloned.1.call-update) | async-done | bytes 147472 | tf_op jit(solution)/shard_map/reduce_scatter | solution.py:222
  903.5 1.6 convert_element_type.169
  905.2 26.6 %reduce-scatter.29.cloned.1.call-done = bf16[384,192]{0,1:T(8,128)(2,1)} async-done(((bf16[384,768]{0,1:T(8,128)(2,1)}), bf16[384,192]{0,1:T(8,128)(2,1)}) %reduce-scatter.29.cloned.1.call-update) | async-done | bytes 147472 | tf_op jit(solution)/shard_map/reduce_scatter | solution.py:228
  931.7 1.6 convert_element_type.171
  933.4 25.0 %reduce-scatter.33.cloned.1.call-done = bf16[192,96]{1,0:T(8,128)(2,1)} async-done(((bf16[768,96]{1,0:T(8,128)(2,1)}), bf16[192,96]{1,0:T(8,128)(2,1)}) %reduce-scatter.33.cloned.1.call-update) | async-done | bytes 36880
  959.9 25.8 %reduce-scatter.23.cloned.1.call-done = bf16[192,96]{1,0:T(8,128)(2,1)} async-done(((bf16[768,96]{1,0:T(8,128)(2,1)}), bf16[192,96]{1,0:T(8,128)(2,1)}) %reduce-scatter.23.cloned.1.call-update) | async-done | bytes 36880 | tf_op jit(solution)/shard_map/reduce_scatter | solution.py:219
  987.1 70.5 %reduce-scatter.21.cloned.1.call-done = bf16[512,768]{1,0:T(8,128)(2,1)} async-done(((bf16[4096,768]{1,0:T(8,128)(2,1)}), bf16[512,768]{1,0:T(8,128)(2,1)}) %reduce-scatter.21.cloned.1.call-update) | async-done | bytes 786448 | tf_op jit(solution)/shard_map/reduce_scatter | solution.py:198
  1057.7 1.6 fusion.62
  1059.3 2.1 fusion.60
  1061.4 9.9 all-reduce.10
  1071.4 13.7 %all-reduce.8 = (bf16[192]{0:T(256)(128)(2,1)S(1)}, bf16[192]{0:T(256)(128)(2,1)S(1)}) all-reduce(bf16[192]{0:T(256)(128)(2,1)S(1)} %dynamic-slice.6, bf16[192]{0:T(256)(128)(2,1)S(1)} %dynamic-slice.10), channel_id=7, replica_groups=mesh['gx'=4,'gy'=8] {'gy'}, use_global_device_ids=true, to_apply=%region_16.17.clone | all-reduce | flops 384 | bytes 1536
  1086.3 3.0 add_add_fusion.2
  1089.3 3.2 reduce-scatter.25.cloned.1.call-done
  1092.5 1.7 convert_element_type.163
  (165 shorter events, 35.6 us)
Async XLA Ops:
  7.2 57.5 %copy-start.27 = (s32[8,512]{1,0:T(8,128)S(1)}, s32[8,512]{1,0:T(8,128)}, u32[]{:S(2)}) copy-start(s32[8,512]{1,0:T(8,128)} %param.11) | copy-start | bytes 49156
  7.2 39.2 %all-gather.6.cloned.1.call-start = ((), (), s32[]{:S(2)}) async-start(), calls=%async_computation.10 | async-start | bytes 1769472 | tf_op jit(solution)/shard_map/all_gather | solution.py:134
  7.9 99.6 %all-gather.10.cloned.1.call-start = ((), (), s32[]{:S(2)}) async-start(), calls=%async_computation.12 | async-start | bytes 7077888 | tf_op jit(solution)/shard_map/all_gather | solution.py:152
  41.1 25.1 %copy-start.23 = (f32[768]{0:T(1024)}, f32[768]{0:T(1024)S(1)}, u32[]{:S(2)}) copy-start(f32[768]{0:T(1024)S(1)} %convert_element_type.135) | copy-start | bytes 9220
  42.4 23.8 %copy-start.25 = (f32[512]{0:T(512)}, f32[512]{0:T(512)S(1)}, u32[]{:S(2)}) copy-start(f32[512]{0:T(512)S(1)} %broadcast_multiply_fusion.1) | copy-start | bytes 6148
  43.9 22.3 %copy-start.31 = (f32[512]{0:T(512)}, f32[512]{0:T(512)S(1)}, u32[]{:S(2)}) copy-start(f32[512]{0:T(512)S(1)} %fusion.61) | copy-start | bytes 6148
  43.9 22.3 %copy-start.29 = (f32[512]{0:T(512)}, f32[512]{0:T(512)S(1)}, u32[]{:S(2)}) copy-start(f32[512]{0:T(512)S(1)} %fusion.100) | copy-start | bytes 6148
  46.3 131.8 %all-gather.8.cloned.1.call-start = ((), (), s32[]{:S(2)}) async-start(), calls=%async_computation.11 | async-start | bytes 7864320 | tf_op jit(solution)/shard_map/all_gather | solution.py:143
  47.0 304.7 %reduce-scatter.15.cloned.1.call-start = ((), (), s32[]{:S(2)}) async-start(), calls=%async_computation.13 | async-start | bytes 14155776 | tf_op jit(solution)/shard_map/reduce_scatter | solution.py:159
  56.4 56.0 %copy-start.18 = (bf16[768,96]{1,0:T(8,128)(2,1)}, bf16[768,96]{1,0:T(8,128)(2,1)S(1)}, u32[]{:S(2)}) copy-start(bf16[768,96]{1,0:T(8,128)(2,1)S(1)} %all_gather.44) | copy-start | bytes 442372
  66.2 130.3 %copy-start.4 = (pred[8,512,512]{1,2,0:T(8,128)(4,1)}, pred[8,512,512]{1,2,0:T(8,128)(4,1)S(1)}, u32[]{:S(2)}) copy-start(pred[8,512,512]{1,2,0:T(8,128)(4,1)S(1)} %broadcast_compare_fusion) | copy-start | bytes 6291460
  189.7 6.8 copy-start.3
  189.7 6.8 copy-start.20
  215.9 6.4 copy-start.6
  222.3 129.4 %copy-start = (bf16[512,768]{1,0:T(8,128)(2,1)S(1)}, bf16[512,768]{1,0:T(8,128)(2,1)}, u32[]{:S(2)}) copy-start(bf16[512,768]{1,0:T(8,128)(2,1)} %param.10) | copy-start | bytes 2359300
  222.3 277.4 %all-gather.12.cloned.1.call-start = ((), (), s32[]{:S(2)}) async-start(), calls=%async_computation.15 | async-start | bytes 7077888 | tf_op jit(solution)/shard_map/all_gather | solution.py:177
  222.9 371.9 %reduce-scatter.19.cloned.1.call-start = ((), (), s32[]{:S(2)}) async-start(), calls=%async_computation.16 | async-start | bytes 7077888 | tf_op jit(solution)/shard_map/reduce_scatter | solution.py:183
  353.9 19.4 %collective-permute-start = (bf16[512,768]{1,0:T(8,128)(2,1)S(1)}, bf16[512,768]{1,0:T(8,128)(2,1)S(1)}, u32[]{:S(2)}, u32[]{:S(2)}) collective-permute-start(bf16[512,768]{1,0:T(8,128)(2,1)S(1)} %multiply_convert_fusion.1), channel_id=1, source_target_pairs={{0,1},{1,2},{2,3},{3,4},{4,5},{5,6},{6,7},{7,0},{8,9},{9,10},{10,1... | collective-permute-start | bytes 2359304 | tf_op jit(solution)/shard_map/ppermute | solution.py:165
  373.3 30.1 %collective-permute-start.1 = (bf16[512,768]{1,0:T(8,128)(2,1)S(1)}, bf16[512,768]{1,0:T(8,128)(2,1)S(1)}, u32[]{:S(2)}, u32[]{:S(2)}) collective-permute-start(bf16[512,768]{1,0:T(8,128)(2,1)S(1)} %collective-permute-done), channel_id=1, source_target_pairs={{0,1},{1,2},{2,3},{3,4},{4,5},{5,6},{6,7},{7,0},{8,9},{9,10},{10,1... | collective-permute-start | bytes 2359304 | tf_op jit(solution)/shard_map/ppermute | solution.py:165
  403.4 0.9 copy-start.10
  404.3 30.0 %collective-permute-start.2 = (bf16[512,768]{1,0:T(8,128)(2,1)S(1)}, bf16[512,768]{1,0:T(8,128)(2,1)S(1)}, u32[]{:S(2)}, u32[]{:S(2)}) collective-permute-start(bf16[512,768]{1,0:T(8,128)(2,1)S(1)} %collective-permute-done.1), channel_id=1, source_target_pairs={{0,1},{1,2},{2,3},{3,4},{4,5},{5,6},{6,7},{7,0},{8,9},{9,10},{10,1... | collective-permute-start | bytes 2359304 | tf_op jit(solution)/shard_map/ppermute | solution.py:165
  434.3 0.9 copy-start.12
  435.2 13.2 %collective-permute-start.3 = (bf16[512,768]{1,0:T(8,128)(2,1)S(1)}, bf16[512,768]{1,0:T(8,128)(2,1)S(1)}, u32[]{:S(2)}, u32[]{:S(2)}) collective-permute-start(bf16[512,768]{1,0:T(8,128)(2,1)S(1)} %collective-permute-done.2), channel_id=1, source_target_pairs={{0,1},{1,2},{2,3},{3,4},{4,5},{5,6},{6,7},{7,0},{8,9},{9,10},{10,1... | collective-permute-start | bytes 2359304 | tf_op jit(solution)/shard_map/ppermute | solution.py:165
  448.4 0.9 copy-start.14
  449.3 13.2 %collective-permute-start.4 = (bf16[512,768]{1,0:T(8,128)(2,1)S(1)}, bf16[512,768]{1,0:T(8,128)(2,1)S(1)}, u32[]{:S(2)}, u32[]{:S(2)}) collective-permute-start(bf16[512,768]{1,0:T(8,128)(2,1)S(1)} %collective-permute-done.3), channel_id=1, source_target_pairs={{0,1},{1,2},{2,3},{3,4},{4,5},{5,6},{6,7},{7,0},{8,9},{9,10},{10,1... | collective-permute-start | bytes 2359304 | tf_op jit(solution)/shard_map/ppermute | solution.py:165
  462.5 0.9 copy-start.16
  463.4 13.3 %collective-permute-start.5 = (bf16[512,768]{1,0:T(8,128)(2,1)S(1)}, bf16[512,768]{1,0:T(8,128)(2,1)}, u32[]{:S(2)}, u32[]{:S(2)}) collective-permute-start(bf16[512,768]{1,0:T(8,128)(2,1)S(1)} %collective-permute-done.4), channel_id=1, source_target_pairs={{0,1},{1,2},{2,3},{3,4},{4,5},{5,6},{6,7},{7,0},{8,9},{9,10},{10,1... | collective-permute-start | bytes 2359304 | tf_op jit(solution)/shard_map/ppermute | solution.py:165
  476.7 28.8 %collective-permute-start.6 = (bf16[512,768]{1,0:T(8,128)(2,1)}, bf16[512,768]{1,0:T(8,128)(2,1)}, u32[]{:S(2)}, u32[]{:S(2)}) collective-permute-start(bf16[512,768]{1,0:T(8,128)(2,1)} %collective-permute-done.5), channel_id=1, source_target_pairs={{0,1},{1,2},{2,3},{3,4},{4,5},{5,6},{6,7},{7,0},{8,9},{9,10},{10,1... | collective-permute-start | bytes 2359304 | tf_op jit(solution)/shard_map/ppermute | solution.py:165
  499.7 8.3 copy-start.17
  499.7 8.4 copy-start.15
  505.5 2.7 copy-start.13
  505.5 2.7 copy-start.11
  509.8 1.8 copy-start.22
  511.6 8.6 copy-start.28
  520.3 1.6 copy-start.33
  527.2 1.1 copy-start.21
  527.3 138.0 %reduce-scatter.17.cloned.1.call-start = ((), (), s32[]{:S(2)}) async-start(), calls=%async_computation.14 | async-start | bytes 7077888 | tf_op jit(solution)/shard_map/reduce_scatter | solution.py:173
  538.4 131.0 %copy-start.7 = (bf16[512,768]{1,0:T(8,128)(2,1)S(1)}, bf16[512,768]{1,0:T(8,128)(2,1)}, u32[]{:S(2)}) copy-start(bf16[512,768]{1,0:T(8,128)(2,1)} %param.19) | copy-start | bytes 2359300
  538.4 195.5 %all-gather.14.cloned.1.call-start = ((), (), s32[]{:S(2)}) async-start(), calls=%async_computation.17 | async-start | bytes 7077888 | tf_op jit(solution)/shard_map/all_gather | solution.py:190
  668.2 1.1 copy-start.1
  670.6 205.1 %reduce-scatter.31.cloned.1.call-start = ((), (), s32[]{:S(2)}) async-start(), calls=%async_computation.23 | async-start | bytes 7864320
  670.7 69.0 %copy-start.5 = (pred[8,512,512]{1,2,0:T(8,128)(4,1)S(1)}, pred[8,512,512]{1,2,0:T(8,128)(4,1)}, u32[]{:S(2)}) copy-start(pred[8,512,512]{1,2,0:T(8,128)(4,1)} %copy-done.4) | copy-start | bytes 6291460
  774.1 3.2 copy-start.9
  806.7 96.9 %reduce-scatter.27.cloned.1.call-start = ((), (), s32[]{:S(2)}) async-start(), calls=%async_computation.21 | async-start | bytes 737280 | tf_op jit(solution)/shard_map/reduce_scatter | solution.py:222
  814.7 117.0 %reduce-scatter.29.cloned.1.call-start = ((), (), s32[]{:S(2)}) async-start(), calls=%async_computation.22 | async-start | bytes 737280 | tf_op jit(solution)/shard_map/reduce_scatter | solution.py:228
  824.0 134.4 %reduce-scatter.33.cloned.1.call-start = ((), (), s32[]{:S(2)}) async-start(), calls=%async_computation.24 | async-start | bytes 245760
  838.4 7.1 copy-start.19
  839.7 146.0 %reduce-scatter.23.cloned.1.call-start = ((), (), s32[]{:S(2)}) async-start(), calls=%async_computation.19 | async-start | bytes 245760 | tf_op jit(solution)/shard_map/reduce_scatter | solution.py:219
  845.5 212.2 %reduce-scatter.21.cloned.1.call-start = ((), (), s32[]{:S(2)}) async-start(), calls=%async_computation.18 | async-start | bytes 7077888 | tf_op jit(solution)/shard_map/reduce_scatter | solution.py:198
  850.0 207.7 %copy-start.24 = (f32[768]{0:T(1024)S(1)}, f32[768]{0:T(1024)}, u32[]{:S(2)}) copy-start(f32[768]{0:T(1024)} %copy-done.23) | copy-start | bytes 9220
  850.0 207.7 %copy-start.26 = (f32[512]{0:T(512)S(1)}, f32[512]{0:T(512)}, u32[]{:S(2)}) copy-start(f32[512]{0:T(512)} %copy-done.25) | copy-start | bytes 6148
  850.1 209.2 %copy-start.32 = (f32[512]{0:T(512)S(1)}, f32[512]{0:T(512)}, u32[]{:S(2)}) copy-start(f32[512]{0:T(512)} %copy-done.31) | copy-start | bytes 6148
  850.1 209.3 %copy-start.30 = (f32[512]{0:T(512)S(1)}, f32[512]{0:T(512)}, u32[]{:S(2)}) copy-start(f32[512]{0:T(512)} %copy-done.29) | copy-start | bytes 6148
  850.1 236.2 %copy-start.2 = (f32[512,768]{1,0:T(8,128)S(1)}, f32[512,768]{1,0:T(8,128)}, u32[]{:S(2)}) copy-start(f32[512,768]{1,0:T(8,128)} %copy-done.1) | copy-start | bytes 4718596
  850.1 236.2 %copy-start.8 = (bf16[512,768]{1,0:T(8,128)(2,1)S(1)}, bf16[512,768]{1,0:T(8,128)(2,1)}, u32[]{:S(2)}) copy-start(bf16[512,768]{1,0:T(8,128)(2,1)} %param.19) | copy-start | bytes 2359300
  850.1 242.4 %reduce-scatter.25.cloned.1.call-start = ((), (), s32[]{:S(2)}) async-start(), calls=%async_computation.20 | async-start | bytes 1769472 | tf_op jit(solution)/shard_map/reduce_scatter | solution.py:242
Sparse Core Ops, SparseCore 0:
  9.6 27.8 all-gather.5
  46.4 61.0 all-gather.9
  109.4 68.6 all-gather.7
  222.4 129.2 reduce-scatter.14
  353.2 83.2 all-gather.11
  527.4 67.3 reduce-scatter.18
  597.1 68.1 reduce-scatter.16
  670.7 63.1 all-gather.13
  806.8 68.8 reduce-scatter.30
  878.4 25.0 reduce-scatter.26
  906.6 25.0 reduce-scatter.28
  934.4 23.9 reduce-scatter.32
  961.7 23.9 reduce-scatter.22
  987.9 69.7 reduce-scatter.20
  1059.8 32.6 reduce-scatter.24
